TPU v7x, 256 devices: a whole 4x4x8 slice. The times are simulated.
256 devices in a mesh: layer: 4 (over y_hi, core), feat: 64 (over y_lo, z, x).
Axes of the slice: x: 4, y: 4 (y_hi: 2, y_lo: 2; y = y_hi * 2 + y_lo), z: 8, core: 2. Of those that a mesh axis runs over, the one named last changes fastest.
Arguments:
- inputs: bfloat16 [768, 4, 2048], P('feat', 'layer'), may hold values from -6 to 6
- w_enc: bfloat16 [4, 2048, 16384], P('layer', None, 'feat'), may hold values from -6 to 6
- b_enc: bfloat16 [16384], P('feat'), may hold values from -3 to 3
- w_dec: bfloat16 [16384, 4, 2048], P('feat', 'layer'), may hold values from -15 to 15
- b_dec: bfloat16 [4, 2048], P('layer'), may hold values from -3 to 3
Outputs:
- recon: bfloat16 [768, 4, 2048], P('feat', 'layer')
- new_enc: float32 [4, 2048, 16384], P('layer', None, 'feat')
- new_dec: float32 [16384, 4, 2048], P('feat', 'layer')
All inputs are finite; a program needn't handle non-finite values.
Results may differ from a plain program's by a relative error of at most 0.0055.
Values may be sent and summed in bfloat16 or wider, within the bound.
No kernel may reach another device: no remote copies, remote signals or barrier semaphores. Data moves between devices by JAX's collectives and lax.ppermute only.
A program may use at most 64 MiB of HBM per device.

v0:
```python
import math
import jax
import jax.numpy as jnp
from jax import lax
from jax.sharding import PartitionSpec as P

D = 2048
F = 16384
L = 4
LEARN_RATE = 1.0
SHRINK_LEVEL = 0.5
EPSILON = 1e-06


def body(inputs, w_enc, b_enc, w_dec, b_dec):
    token_rows, layer_count, model_width = inputs.shape
    feature_count = w_enc.shape[2]
    flat_width = layer_count * model_width
    scale_enc = 1.0 / math.sqrt(L * D)
    scale_dec = 1.0 / math.sqrt(F)
    x_local = inputs.reshape(token_rows, flat_width)
    x_all = lax.all_gather(x_local, "feat", axis=0, tiled=True)
    enc_mat = w_enc.reshape(flat_width, feature_count)
    dec_mat = w_dec.reshape(feature_count, flat_width)
    pre_part = jnp.dot(x_all, enc_mat, preferred_element_type=jnp.float32)
    pre_act = lax.psum(pre_part, "layer") * scale_enc + b_enc.astype(jnp.float32)
    latent = jnp.maximum(pre_act, 0.0).astype(jnp.bfloat16)
    bias_flat = b_dec.reshape(flat_width).astype(jnp.float32)
    summed = lax.psum_scatter(
        jnp.dot(latent, dec_mat, preferred_element_type=jnp.float32),
        "feat",
        scatter_dimension=0,
        tiled=True,
    )
    recon_local = summed * scale_dec + bias_flat
    err_local = (recon_local - x_local.astype(jnp.float32)).astype(jnp.bfloat16)
    err_all = lax.all_gather(err_local, "feat", axis=0, tiled=True)
    recon = recon_local.astype(jnp.bfloat16).reshape(token_rows, layer_count, model_width)
    grad_part = lax.dot_general(
        err_all, dec_mat, (((1,), (1,)), ((), ())), preferred_element_type=jnp.float32
    )
    grad_dec = (
        lax.dot_general(
            latent, err_all, (((0,), (0,)), ((), ())), preferred_element_type=jnp.float32
        )
        * scale_dec
    )
    half_dec = dec_mat.astype(jnp.float32) - LEARN_RATE * grad_dec
    square_part = jnp.sum(half_dec * half_dec, axis=1)
    grad_sum, square_sum = (
        lax.psum(grad_part.astype(jnp.bfloat16), "layer").astype(jnp.float32),
        lax.psum(square_part.astype(jnp.bfloat16), "layer").astype(jnp.float32),
    )
    grad_latent = grad_sum * scale_dec
    grad_pre = jnp.where(pre_act > 0.0, grad_latent, 0.0).astype(jnp.bfloat16)
    grad_enc = (
        lax.dot_general(
            x_all, grad_pre, (((0,), (0,)), ((), ())), preferred_element_type=jnp.float32
        )
        * scale_enc
    )
    new_enc = (enc_mat.astype(jnp.float32) - LEARN_RATE * grad_enc).reshape(
        layer_count, model_width, feature_count
    )
    row_rms = jnp.sqrt(square_sum / (L * D) + EPSILON)
    factor = jnp.maximum(0.0, 1.0 - SHRINK_LEVEL / row_rms)
    new_dec = (half_dec * factor[:, None]).reshape(feature_count, layer_count, model_width)
    return (recon, new_enc, new_dec)


def solution(mesh):
    return jax.shard_map(
        body,
        mesh=mesh,
        in_specs=(
            P("feat", "layer", None),
            P("layer", None, "feat"),
            P("feat"),
            P("feat", "layer", None),
            P("layer", None),
        ),
        out_specs=(P("feat", "layer", None), P("layer", None, "feat"), P("feat", "layer", None)),
        check_vma=False,
    )
```

profile of v0, /device:TPU:1, one launch (start us, length us, event | category | flops | bytes accessed | tf_op | source)
XLA Modules:
  0.0 1049.1 jit_solution(5644969104625668437)
XLA Ops:
  7.2 0.0 all-gather.5.cloned.1.call-start
  7.2 1.6 copy.18
  8.8 0.0 all-gather.5.cloned.1.call-update
  8.8 0.0 copy-start.22
  8.8 0.0 copy-start.2
  8.8 0.0 all-reduce.5.cloned.1.call-start
  8.9 267.4 %all-gather.5.cloned.1.call-done = bf16[768,1,2048]{2,1,0:T(2,128)(2,1)} async-done(((bf16[12,1,2048]{2,1,0:T(2,128)(2,1)}), bf16[768,1,2048]{2,1,0:T(2,128)(2,1)}) %all-gather.5.cloned.1.call-update) | async-done | bytes 3145744 | tf_op jit(solution)/shard_map/all_gather | solution.py:22
  276.2 5.8 fusion.3
  282.0 0.0 all-reduce.5.cloned.1.call-update
  282.0 0.0 all-gather.7.cloned.1.call-start
  282.1 91.4 %all-reduce.5.cloned.1.call-done = f32[768,256]{1,0:T(8,128)} async-done(((f32[768,256]{1,0:T(8,128)}), f32[768,256]{1,0:T(8,128)}) %all-reduce.5.cloned.1.call-update) | async-done | bytes 786448 | tf_op jit(solution)/shard_map/psum | solution.py:26
  373.5 4.7 fusion.22
  378.2 162.5 %fusion = f32[16,2048]{1,0:T(8,128)S(1)} fusion(f32[768,2048]{1,0:T(8,128)} %fusion.22), kind=kCustom, calls=%all-reduce-scatter | all-reduce-scatter fusion | flops 2097153 | bytes 6423552
  540.8 0.0 copy-start.4
  540.8 0.0 copy-start.1
  540.8 1.4 collective-permute-start.15
  542.3 1.3 collective-permute-start
  543.6 1.3 collective-permute-start.1
  544.9 6.4 collective-permute-start.10
  551.3 3.7 collective-permute-start.11
  555.1 0.0 collective-permute-done.15
  555.1 0.0 copy-start.5
  555.1 7.0 collective-permute-start.12
  562.1 0.0 collective-permute-done
  562.2 1.6 collective-permute-start.13
  563.8 0.0 collective-permute-done.1
  563.8 4.3 collective-permute-start.14
  568.1 0.0 collective-permute-done.10
  568.2 5.8 collective-permute-start.2
  574.0 0.0 collective-permute-done.11
  574.0 1.3 collective-permute-start.3
  575.3 0.0 collective-permute-done.12
  575.3 4.1 collective-permute-start.4
  579.4 0.0 collective-permute-done.13
  579.4 3.3 collective-permute-start.5
  582.8 0.0 copy-start.12
  582.8 8.8 collective-permute-start.6
  591.6 0.0 collective-permute-done.2
  591.6 3.1 collective-permute-start.7
  594.7 4.4 collective-permute-start.8
  599.1 0.0 collective-permute-done.4
  599.2 2.6 collective-permute-start.9
  601.9 0.6 dynamic-slice.4
  603.1 0.0 collective-permute-done.5
  603.2 0.0 collective-permute-done.7
  603.2 1.0 collective-permute-done.8
  604.2 0.6 copy-done.19
  604.8 7.7 collective-permute-done.9
  612.5 16.4 %concatenate = f32[268,2048]{1,0:T(8,128)S(1)} concatenate(f32[12,2048]{1,0:T(8,128)} %copy-done.5, f32[16,2048]{1,0:T(8,128)} %copy-done.12, f32[16,2048]{1,0:T(8,128)} %copy-done.11, f32[16,2048]{1,0:T(8,128)} %copy-done.10, f32[16,2048]{1,0:T(8,128)} %copy-done.9, f32[16,2048]{1,0:T(8,128)} %copy-done.8, f32[16,2048]{1,0:T(8,128)} %collective-permute-done.9, ...), dimensions={0} | concatenate | bytes 4390912
  628.9 0.7 fusion.32
  629.6 0.0 all-gather.7.cloned.1.call-update
  629.6 0.0 all-reduce.7.cloned.1.call-start
  629.7 1.4 copy.19
  631.1 292.3 %all-gather.7.cloned.1.call-done = bf16[64,12,2048]{2,1,0:T(8,128)(2,1)} async-done(((bf16[1,12,2048]{2,1,0:T(8,128)(2,1)}), bf16[64,12,2048]{2,1,0:T(8,128)(2,1)}) %all-gather.7.cloned.1.call-update) | async-done | bytes 3145744 | tf_op jit(solution)/shard_map/all_gather | solution.py:37
  923.5 6.2 reshape.37
  929.6 3.7 convolution_convert_fusion
  933.4 3.3 multiply_reduce_fusion
  936.7 53.0 %psum.23 = bf16[256]{0:T(256)(128)(2,1)S(1)} all-reduce(bf16[256]{0:T(256)(128)(2,1)S(1)} %get-tuple-element.17), channel_id=1, replica_groups=mesh['layer'=4,'feat'=64] {'layer'}, use_global_device_ids=true, to_apply=%region_4.0 | all-reduce | flops 256 | bytes 1024 | tf_op jit(solution)/shard_map/psum | solution.py:52
  989.8 0.0 all-reduce.7.cloned.1.call-update
  989.8 0.2 multiply_bitcast_fusion
  990.0 3.5 copy.21
  993.5 41.8 %all-reduce.7.cloned.1.call-done = bf16[768,256]{1,0:T(8,128)(2,1)} async-done(((bf16[768,256]{1,0:T(8,128)(2,1)}), bf16[768,256]{1,0:T(8,128)(2,1)}) %all-reduce.7.cloned.1.call-update) | async-done | bytes 393232 | tf_op jit(solution)/shard_map/psum | solution.py:51
  1035.3 5.5 fusion.14
  1040.8 1.8 copy.20
  (46 shorter events, 0.1 us)
Async XLA Ops:
  7.2 269.1 %all-gather.5.cloned.1.call-start = ((), (), s32[]{:S(2)}) async-start(), calls=%async_computation.2 | async-start | bytes 6389760 | tf_op jit(solution)/shard_map/all_gather | solution.py:22
  8.8 273.3 %copy-start.22 = (bf16[256]{0:T(256)(128)(2,1)S(1)}, bf16[256]{0:T(256)(128)(2,1)}, u32[]{:S(2)}) copy-start(bf16[256]{0:T(256)(128)(2,1)} %param.7) | copy-start | bytes 1540
  8.8 364.7 %copy-start.2 = (bf16[256,1,2048]{2,0,1:T(8,128)(2,1)S(1)}, bf16[256,1,2048]{2,0,1:T(8,128)(2,1)}, u32[]{:S(2)}) copy-start(bf16[256,1,2048]{2,0,1:T(8,128)(2,1)} %param.8) | copy-start | bytes 3145732
  8.8 364.7 %all-reduce.5.cloned.1.call-start = ((), (), s32[]{:S(2)}) async-start(), calls=%async_computation | async-start | bytes 1572864 | tf_op jit(solution)/shard_map/psum | solution.py:26
  282.0 641.4 %all-gather.7.cloned.1.call-start = ((), (), s32[]{:S(2)}) async-start(), calls=%async_computation.3 | async-start | bytes 4259840 | tf_op jit(solution)/shard_map/all_gather | solution.py:37
  378.2 223.6 %copy-start.20 = (bf16[1,2048]{1,0:T(2,128)(2,1)S(1)}, bf16[1,2048]{1,0:T(2,128)(2,1)}, u32[]{:S(2)}) copy-start(bf16[1,2048]{1,0:T(2,128)(2,1)} %param.9) | copy-start | bytes 12292
  378.2 223.6 %copy-start.21 = (u32[256]{0:T(256)S(1)}, u32[256]{0:T(256)}, u32[]{:S(2)}) copy-start(u32[256]{0:T(256)} %constant.26) | copy-start | bytes 3076
  540.8 88.1 %copy-start.4 = (bf16[12,1,2048]{2,0,1:T(8,128)(2,1)S(1)}, bf16[12,1,2048]{2,0,1:T(8,128)(2,1)}, u32[]{:S(2)}) copy-start(bf16[12,1,2048]{2,0,1:T(8,128)(2,1)} %param.5) | copy-start | bytes 147460
  540.8 88.9 %copy-start.1 = (bf16[1,2048,256]{2,1,0:T(8,128)(2,1)S(1)}, bf16[1,2048,256]{2,1,0:T(8,128)(2,1)}, u32[]{:S(2)}) copy-start(bf16[1,2048,256]{2,1,0:T(8,128)(2,1)} %param.6) | copy-start | bytes 3145732
  540.8 14.2 %collective-permute-start.15 = (f32[12,2048]{1,0:T(8,128)S(1)}, f32[12,2048]{1,0:T(8,128)S(1)}, u32[]{:S(2)}, u32[]{:S(2)}) collective-permute-start(f32[12,2048]{1,0:T(8,128)S(1)} %slice), channel_id=1, source_target_pairs={{0,16},{1,17},{2,18},{3,19},{4,20},{5,21},{6,22},{7,23},{8,24},{9,... | collective-permute-start | bytes 294920
  542.3 19.9 %collective-permute-start = (f32[16,2048]{1,0:T(8,128)S(1)}, f32[16,2048]{1,0:T(8,128)S(1)}, u32[]{:S(2)}, u32[]{:S(2)}) collective-permute-start(f32[16,2048]{1,0:T(8,128)S(1)} %fusion), channel_id=1, source_target_pairs={{0,1},{1,2},{2,3},{3,4},{4,5},{5,6},{6,7},{7,8},{8,9},{9,10},{10,1... | collective-permute-start | bytes 393224
  543.6 20.2 %collective-permute-start.1 = (f32[16,2048]{1,0:T(8,128)S(1)}, f32[16,2048]{1,0:T(8,128)S(1)}, u32[]{:S(2)}, u32[]{:S(2)}) collective-permute-start(f32[16,2048]{1,0:T(8,128)S(1)} %fusion), channel_id=1, source_target_pairs={{0,2},{1,3},{2,4},{3,5},{4,6},{5,7},{6,8},{7,9},{8,10},{9,11},{10,... | collective-permute-start | bytes 393224
  544.9 23.3 %collective-permute-start.10 = (f32[16,2048]{1,0:T(8,128)S(1)}, f32[16,2048]{1,0:T(8,128)S(1)}, u32[]{:S(2)}, u32[]{:S(2)}) collective-permute-start(f32[16,2048]{1,0:T(8,128)S(1)} %fusion), channel_id=1, source_target_pairs={{0,11},{1,12},{2,13},{3,14},{4,15},{5,16},{6,17},{7,18},{8,19},{9,... | collective-permute-start | bytes 393224
  551.3 22.6 %collective-permute-start.11 = (f32[16,2048]{1,0:T(8,128)S(1)}, f32[16,2048]{1,0:T(8,128)S(1)}, u32[]{:S(2)}, u32[]{:S(2)}) collective-permute-start(f32[16,2048]{1,0:T(8,128)S(1)} %fusion), channel_id=1, source_target_pairs={{0,12},{1,13},{2,14},{3,15},{4,16},{5,17},{6,18},{7,19},{8,20},{9,... | collective-permute-start | bytes 393224
  555.1 44.0 %copy-start.5 = (f32[12,2048]{1,0:T(8,128)}, f32[12,2048]{1,0:T(8,128)S(1)}, u32[]{:S(2)}) copy-start(f32[12,2048]{1,0:T(8,128)S(1)} %collective-permute-done.15) | copy-start | bytes 294916
  555.1 20.2 %collective-permute-start.12 = (f32[16,2048]{1,0:T(8,128)S(1)}, f32[16,2048]{1,0:T(8,128)S(1)}, u32[]{:S(2)}, u32[]{:S(2)}) collective-permute-start(f32[16,2048]{1,0:T(8,128)S(1)} %fusion), channel_id=1, source_target_pairs={{0,13},{1,14},{2,15},{3,16},{4,17},{5,18},{6,19},{7,20},{8,21},{9,... | collective-permute-start | bytes 393224
  562.1 39.6 %copy-start.6 = (f32[16,2048]{1,0:T(8,128)}, f32[16,2048]{1,0:T(8,128)S(1)}, u32[]{:S(2)}) copy-start(f32[16,2048]{1,0:T(8,128)S(1)} %collective-permute-done) | copy-start | bytes 393220
  562.2 17.3 %collective-permute-start.13 = (f32[16,2048]{1,0:T(8,128)S(1)}, f32[16,2048]{1,0:T(8,128)S(1)}, u32[]{:S(2)}, u32[]{:S(2)}) collective-permute-start(f32[16,2048]{1,0:T(8,128)S(1)} %fusion), channel_id=1, source_target_pairs={{0,14},{1,15},{2,16},{3,17},{4,18},{5,19},{6,20},{7,21},{8,22},{9,... | collective-permute-start | bytes 393224
  563.8 37.9 %copy-start.7 = (f32[16,2048]{1,0:T(8,128)}, f32[16,2048]{1,0:T(8,128)S(1)}, u32[]{:S(2)}) copy-start(f32[16,2048]{1,0:T(8,128)S(1)} %collective-permute-done.1) | copy-start | bytes 393220
  563.8 18.9 %collective-permute-start.14 = (f32[16,2048]{1,0:T(8,128)S(1)}, f32[16,2048]{1,0:T(8,128)S(1)}, u32[]{:S(2)}, u32[]{:S(2)}) collective-permute-start(f32[16,2048]{1,0:T(8,128)S(1)} %fusion), channel_id=1, source_target_pairs={{0,15},{1,16},{2,17},{3,18},{4,19},{5,20},{6,21},{7,22},{8,23},{9,... | collective-permute-start | bytes 393224
  568.2 33.6 %copy-start.8 = (f32[16,2048]{1,0:T(8,128)}, f32[16,2048]{1,0:T(8,128)S(1)}, u32[]{:S(2)}) copy-start(f32[16,2048]{1,0:T(8,128)S(1)} %collective-permute-done.10) | copy-start | bytes 393220
  568.2 23.5 %collective-permute-start.2 = (f32[16,2048]{1,0:T(8,128)S(1)}, f32[16,2048]{1,0:T(8,128)S(1)}, u32[]{:S(2)}, u32[]{:S(2)}) collective-permute-start(f32[16,2048]{1,0:T(8,128)S(1)} %fusion), channel_id=1, source_target_pairs={{0,3},{1,4},{2,5},{3,6},{4,7},{5,8},{6,9},{7,10},{8,11},{9,12},{10... | collective-permute-start | bytes 393224
  574.0 27.8 %copy-start.9 = (f32[16,2048]{1,0:T(8,128)}, f32[16,2048]{1,0:T(8,128)S(1)}, u32[]{:S(2)}) copy-start(f32[16,2048]{1,0:T(8,128)S(1)} %collective-permute-done.11) | copy-start | bytes 393220
  574.0 20.7 %collective-permute-start.3 = (f32[16,2048]{1,0:T(8,128)S(1)}, f32[16,2048]{1,0:T(8,128)S(1)}, u32[]{:S(2)}, u32[]{:S(2)}) collective-permute-start(f32[16,2048]{1,0:T(8,128)S(1)} %fusion), channel_id=1, source_target_pairs={{0,4},{1,5},{2,6},{3,7},{4,8},{5,9},{6,10},{7,11},{8,12},{9,13},{1... | collective-permute-start | bytes 393224
  575.3 26.5 %copy-start.10 = (f32[16,2048]{1,0:T(8,128)}, f32[16,2048]{1,0:T(8,128)S(1)}, u32[]{:S(2)}) copy-start(f32[16,2048]{1,0:T(8,128)S(1)} %collective-permute-done.12) | copy-start | bytes 393220
  575.3 23.8 %collective-permute-start.4 = (f32[16,2048]{1,0:T(8,128)S(1)}, f32[16,2048]{1,0:T(8,128)S(1)}, u32[]{:S(2)}, u32[]{:S(2)}) collective-permute-start(f32[16,2048]{1,0:T(8,128)S(1)} %fusion), channel_id=1, source_target_pairs={{0,5},{1,6},{2,7},{3,8},{4,9},{5,10},{6,11},{7,12},{8,13},{9,14},{... | collective-permute-start | bytes 393224
  579.4 22.4 %copy-start.11 = (f32[16,2048]{1,0:T(8,128)}, f32[16,2048]{1,0:T(8,128)S(1)}, u32[]{:S(2)}) copy-start(f32[16,2048]{1,0:T(8,128)S(1)} %collective-permute-done.13) | copy-start | bytes 393220
  579.4 23.7 %collective-permute-start.5 = (f32[16,2048]{1,0:T(8,128)S(1)}, f32[16,2048]{1,0:T(8,128)S(1)}, u32[]{:S(2)}, u32[]{:S(2)}) collective-permute-start(f32[16,2048]{1,0:T(8,128)S(1)} %fusion), channel_id=1, source_target_pairs={{0,6},{1,7},{2,8},{3,9},{4,10},{5,11},{6,12},{7,13},{8,14},{9,15},... | collective-permute-start | bytes 393224
  582.8 19.0 %copy-start.12 = (f32[16,2048]{1,0:T(8,128)}, f32[16,2048]{1,0:T(8,128)S(1)}, u32[]{:S(2)}) copy-start(f32[16,2048]{1,0:T(8,128)S(1)} %collective-permute-done.14) | copy-start | bytes 393220
  582.8 20.4 %collective-permute-start.6 = (f32[16,2048]{1,0:T(8,128)S(1)}, f32[16,2048]{1,0:T(8,128)S(1)}, u32[]{:S(2)}, u32[]{:S(2)}) collective-permute-start(f32[16,2048]{1,0:T(8,128)S(1)} %fusion), channel_id=1, source_target_pairs={{0,7},{1,8},{2,9},{3,10},{4,11},{5,12},{6,13},{7,14},{8,15},{9,16}... | collective-permute-start | bytes 393224
  591.6 10.2 copy-start.13
  591.6 11.5 %collective-permute-start.7 = (f32[16,2048]{1,0:T(8,128)S(1)}, f32[16,2048]{1,0:T(8,128)S(1)}, u32[]{:S(2)}, u32[]{:S(2)}) collective-permute-start(f32[16,2048]{1,0:T(8,128)S(1)} %fusion), channel_id=1, source_target_pairs={{0,8},{1,9},{2,10},{3,11},{4,12},{5,13},{6,14},{7,15},{8,16},{9,17... | collective-permute-start | bytes 393224
  594.7 7.1 copy-start.14
  594.7 9.4 collective-permute-start.8
  599.1 2.7 copy-start.15
  599.2 13.3 %collective-permute-start.9 = (f32[16,2048]{1,0:T(8,128)S(1)}, f32[16,2048]{1,0:T(8,128)}, u32[]{:S(2)}, u32[]{:S(2)}) collective-permute-start(f32[16,2048]{1,0:T(8,128)S(1)} %fusion), channel_id=1, source_target_pairs={{0,10},{1,11},{2,12},{3,13},{4,14},{5,15},{6,16},{7,17},{8,18},{9,... | collective-permute-start | bytes 393224
  603.1 1.0 copy-start.16
  603.1 1.0 copy-start.17
  603.2 1.0 copy-start.18
  604.2 0.7 copy-start.19
  629.6 405.7 %all-reduce.7.cloned.1.call-start = ((), (), s32[]{:S(2)}) async-start(), calls=%async_computation.1 | async-start | bytes 786432 | tf_op jit(solution)/shard_map/psum | solution.py:51
  631.1 298.5 %copy-start.3 = (bf16[256,1,2048]{2,0,1:T(8,128)(2,1)S(1)}, bf16[256,1,2048]{2,0,1:T(8,128)(2,1)}, u32[]{:S(2)}) copy-start(bf16[256,1,2048]{2,0,1:T(8,128)(2,1)} %param.8) | copy-start | bytes 3145732
  929.6 3.7 copy-start
Sparse Core Ops, SparseCore 0:
  10.3 265.8 all-gather.4
  282.2 91.2 all-reduce.4
  629.7 293.6 all-gather.6
  989.9 45.3 all-reduce.6
where the time goes:
time: 1050 us
  waiting for transfers between devices  702 us (67%)
  blocking collectives  216 us (21%)
  starting transfers between devices  60.7 us (6%)
  local copies, waits for them, and re-layouts  32.2 us (3%)
  matrix products  23.1 us (2%)
  between operations  15 us (1%)
    all_gather x1, waiting for transfers between devices, body(): err_all = lax.all_gather(err_local, 'feat', axis=0, tiled=True)  292 us
    all_gather x1, waiting for transfers between devices, body(): x_all = lax.all_gather(x_local, 'feat', axis=0, tiled=True)  267 us
    unnamed x1, blocking collectives  163 us
    psum x1, waiting for transfers between devices, body(): lax.psum(pre_part, 'layer') * scale_enc + b_enc.astype(jnp.float32)  91.4 us
    unnamed x16, starting transfers between devices  60.6 us
    psum x1, blocking collectives, body(): lax.psum(square_part.astype(jnp.bfloat16), 'layer').astype(jnp.float32)  53 us
    psum x1, waiting for transfers between devices, body(): lax.psum(grad_part.astype(jnp.bfloat16), 'layer').astype(jnp.float32)  41.8 us
    unnamed x54, local copies, waits for them, and re-layouts  32.2 us
  transfers between devices with their start and end apart: 20, of which 6 were waited for; matrix products, arithmetic and copies ran while one was open for 1% of the time, Pallas kernels for 0%

commit v1 on v0

--- a/solution.py
+++ b/solution.py
@@ -19,7 +19,9 @@
     scale_enc = 1.0 / math.sqrt(L * D)
     scale_dec = 1.0 / math.sqrt(F)
     x_local = inputs.reshape(token_rows, flat_width)
-    x_all = lax.all_gather(x_local, "feat", axis=0, tiled=True)
+    x_all = jnp.concatenate(
+        lax.all_to_all(jnp.stack([x_local] * lax.axis_size("feat")), "feat", 0, 0), axis=0
+    )
     enc_mat = w_enc.reshape(flat_width, feature_count)
     dec_mat = w_dec.reshape(feature_count, flat_width)
     pre_part = jnp.dot(x_all, enc_mat, preferred_element_type=jnp.float32)

time: 1050 us -> 865 us (0.82)
  waiting for transfers between devices: 702 us -> 391 us
  blocking collectives: 216 us -> 323 us
  local copies, waits for them, and re-layouts: 32.2 us -> 49 us
    all_gather x1 -> x0, waiting for transfers between devices: 267 us -> none  [body(): x_all = lax.all_gather(x_local, 'feat', axis=0, tiled=True)]
    all_to_all x0 -> x1, blocking collectives: none -> 106 us  [body(): lax.all_to_all(jnp.stack([x_local] * lax.axis_size('feat')), 'feat', 0, 0)]
    psum x1, waiting for transfers between devices: 91.4 us -> 49.7 us  [body(): lax.psum(pre_part, 'layer') * scale_enc + b_enc.astype(jnp.float32)]
    unnamed x54 -> x35, local copies, waits for them, and re-layouts: 32.2 us -> 42.9 us
  transfers between devices with their start and end apart: 20 -> 19, of which waited for: 6 -> 5; matrix products, arithmetic and copies ran while one was open for 1% -> 1% of each run, Pallas kernels for 0% -> 0%
where the time goes in v1:
time: 865 us; the launch traced here: 863 us
  waiting for transfers between devices  391 us (45%)
  blocking collectives  323 us (37%)
  starting transfers between devices  61.2 us (7%)
  local copies, waits for them, and re-layouts  49 us (6%)
  matrix products  20.9 us (2%)
  between operations  14.8 us (2%)
    all_gather x1, waiting for transfers between devices, body(): err_all = lax.all_gather(err_local, 'feat', axis=0, tiled=True)  292 us
    unnamed x1, blocking collectives  163 us
    all_to_all x1, blocking collectives, body(): lax.all_to_all(jnp.stack([x_local] * lax.axis_size('feat')), 'feat', 0, 0)  106 us
    unnamed x16, starting transfers between devices  61.1 us
    psum x1, blocking collectives, body(): lax.psum(square_part.astype(jnp.bfloat16), 'layer').astype(jnp.float32)  53 us
    psum x1, waiting for transfers between devices, body(): lax.psum(pre_part, 'layer') * scale_enc + b_enc.astype(jnp.float32)  49.7 us
    unnamed x35, local copies, waits for them, and re-layouts  42.9 us
    psum x1, waiting for transfers between devices, body(): lax.psum(grad_part.astype(jnp.bfloat16), 'layer').astype(jnp.float32)  40.2 us
  transfers between devices with their start and end apart: 19, of which 5 were waited for; matrix products, arithmetic and copies ran while one was open for 1% of the time, Pallas kernels for 0%

profile of v1, /device:TPU:1, one launch (start us, length us, event | category | flops | bytes accessed | tf_op | source)
XLA Modules:
  0.0 863.3 jit_solution(12469626403897135807)
XLA Ops:
  7.2 0.0 all-reduce.5.cloned.1.call-start
  7.2 1.4 stack.3
  8.6 106.3 %all_to_all.5 = bf16[64,12,2048]{2,1,0:T(8,128)(2,1)} all-to-all(bf16[64,12,2048]{2,1,0:T(8,128)(2,1)S(1)} %stack.3), channel_id=1, replica_groups=mesh['layer'=4,'feat'=64] {'feat'}, dimensions={0} | all-to-all | bytes 6291456 | tf_op jit(solution)/shard_map/all_to_all | solution.py:23
  114.9 4.7 reshape.30
  119.6 0.0 copy-start.13
  119.6 3.1 fusion.5
  122.7 0.0 all-reduce.5.cloned.1.call-update
  122.7 0.0 all-gather.3.cloned.1.call-start
  122.8 0.0 copy-done.13
  122.8 49.7 %all-reduce.5.cloned.1.call-done = f32[768,256]{1,0:T(8,128)} async-done(((f32[768,256]{1,0:T(8,128)}), f32[768,256]{1,0:T(8,128)}) %all-reduce.5.cloned.1.call-update) | async-done | bytes 786448 | tf_op jit(solution)/shard_map/psum | solution.py:28
  172.5 5.1 fusion.8
  177.6 163.3 %fusion = f32[16,2048]{1,0:T(8,128)S(1)} fusion(f32[768,2048]{1,0:T(8,128)} %fusion.8), kind=kCustom, calls=%all-reduce-scatter | all-reduce-scatter fusion | flops 2097153 | bytes 6423552
  340.8 0.0 copy-start
  340.9 1.3 collective-permute-start.15
  342.2 1.3 collective-permute-start
  343.5 1.3 collective-permute-start.1
  344.8 5.8 collective-permute-start.10
  350.6 4.0 collective-permute-start.11
  354.6 0.0 collective-permute-done.15
  354.6 7.0 collective-permute-start.12
  361.6 0.0 collective-permute-done
  361.7 0.0 copy-start.1
  361.7 1.6 collective-permute-start.13
  363.3 0.0 collective-permute-done.1
  363.3 4.3 collective-permute-start.14
  367.6 0.0 collective-permute-done.10
  367.7 6.2 collective-permute-start.2
  373.8 0.0 collective-permute-done.11
  373.9 1.3 collective-permute-start.3
  375.2 0.0 collective-permute-done.12
  375.2 3.0 collective-permute-start.4
  378.2 0.0 collective-permute-done.13
  378.2 0.0 copy-start.6
  378.2 4.5 collective-permute-start.5
  382.8 0.0 collective-permute-done.14
  382.8 8.4 collective-permute-start.6
  391.1 0.0 collective-permute-done.2
  391.1 3.0 collective-permute-start.7
  394.1 0.0 collective-permute-done.3
  394.1 6.2 collective-permute-start.8
  400.3 0.0 collective-permute-done.4
  400.3 1.9 collective-permute-start.9
  402.4 0.6 dynamic-slice.4
  403.6 0.0 collective-permute-done.5
  403.6 0.0 collective-permute-done.6
  403.6 0.0 collective-permute-done.7
  403.6 2.5 collective-permute-done.8
  406.1 7.0 collective-permute-done.9
  413.1 27.5 %concatenate = f32[268,2048]{1,0:T(8,128)} concatenate(f32[12,2048]{1,0:T(8,128)S(1)} %collective-permute-done.15, f32[16,2048]{1,0:T(8,128)} %copy-done.7, f32[16,2048]{1,0:T(8,128)} %copy-done.6, f32[16,2048]{1,0:T(8,128)} %copy-done.5, f32[16,2048]{1,0:T(8,128)} %copy-done.4, f32[16,2048]{1,0:T(8,128)} %copy-done.3, f32[16,2048]{1,0:T(8,128)} %collective-permute-done.9, ...), dimensions={0} | concatenate | bytes 4390912
  440.6 1.6 fusion.17
  442.2 0.0 all-gather.3.cloned.1.call-update
  442.2 0.0 all-reduce.7.cloned.1.call-start
  442.3 2.3 copy.14
  444.6 291.9 %all-gather.3.cloned.1.call-done = bf16[64,12,2048]{2,1,0:T(8,128)(2,1)} async-done(((bf16[1,12,2048]{2,1,0:T(8,128)(2,1)}), bf16[64,12,2048]{2,1,0:T(8,128)(2,1)}) %all-gather.3.cloned.1.call-update) | async-done | bytes 3145744 | tf_op jit(solution)/shard_map/all_gather | solution.py:39
  736.4 6.2 reshape.38
  742.6 3.9 convolution_convert_fusion
  746.5 4.8 multiply_reduce_fusion
  751.3 53.0 %psum.23 = bf16[256]{0:T(256)(128)(2,1)S(1)} all-reduce(bf16[256]{0:T(256)(128)(2,1)S(1)} %get-tuple-element.14), channel_id=1, replica_groups=mesh['layer'=4,'feat'=64] {'layer'}, use_global_device_ids=true, to_apply=%region_4.0 | all-reduce | flops 256 | bytes 1024 | tf_op jit(solution)/shard_map/psum | solution.py:54
  804.4 0.0 all-reduce.7.cloned.1.call-update
  804.4 1.8 multiply_bitcast_fusion
  806.2 3.5 copy.16
  809.7 40.2 %all-reduce.7.cloned.1.call-done = bf16[768,256]{1,0:T(8,128)(2,1)} async-done(((bf16[768,256]{1,0:T(8,128)(2,1)}), bf16[768,256]{1,0:T(8,128)(2,1)}) %all-reduce.7.cloned.1.call-update) | async-done | bytes 393232 | tf_op jit(solution)/shard_map/psum | solution.py:53
  849.9 4.0 fusion.4
  853.9 2.9 copy.15
  (27 shorter events, 0.1 us)
Async XLA Ops:
  7.2 165.3 %all-reduce.5.cloned.1.call-start = ((), (), s32[]{:S(2)}) async-start(), calls=%async_computation.1 | async-start | bytes 1572864 | tf_op jit(solution)/shard_map/psum | solution.py:28
  119.6 3.2 copy-start.13
  122.7 613.7 %all-gather.3.cloned.1.call-start = ((), (), s32[]{:S(2)}) async-start(), calls=%async_computation.3 | async-start | bytes 4259840 | tf_op jit(solution)/shard_map/all_gather | solution.py:39
  177.6 224.8 %copy-start.11 = (bf16[1,2048]{1,0:T(2,128)(2,1)S(1)}, bf16[1,2048]{1,0:T(2,128)(2,1)}, u32[]{:S(2)}) copy-start(bf16[1,2048]{1,0:T(2,128)(2,1)} %param.9) | copy-start | bytes 12292
  177.6 224.8 %copy-start.12 = (u32[256]{0:T(256)S(1)}, u32[256]{0:T(256)}, u32[]{:S(2)}) copy-start(u32[256]{0:T(256)} %constant.26) | copy-start | bytes 3076
  340.8 99.7 %copy-start = (bf16[12,1,2048]{2,0,1:T(8,128)(2,1)S(1)}, bf16[12,1,2048]{2,0,1:T(8,128)(2,1)}, u32[]{:S(2)}) copy-start(bf16[12,1,2048]{2,0,1:T(8,128)(2,1)} %param.5) | copy-start | bytes 147460
  340.9 13.7 %collective-permute-start.15 = (f32[12,2048]{1,0:T(8,128)S(1)}, f32[12,2048]{1,0:T(8,128)S(1)}, u32[]{:S(2)}, u32[]{:S(2)}) collective-permute-start(f32[12,2048]{1,0:T(8,128)S(1)} %slice), channel_id=1, source_target_pairs={{0,16},{1,17},{2,18},{3,19},{4,20},{5,21},{6,22},{7,23},{8,24},{9,... | collective-permute-start | bytes 294920
  342.2 19.5 %collective-permute-start = (f32[16,2048]{1,0:T(8,128)S(1)}, f32[16,2048]{1,0:T(8,128)S(1)}, u32[]{:S(2)}, u32[]{:S(2)}) collective-permute-start(f32[16,2048]{1,0:T(8,128)S(1)} %fusion), channel_id=1, source_target_pairs={{0,1},{1,2},{2,3},{3,4},{4,5},{5,6},{6,7},{7,8},{8,9},{9,10},{10,1... | collective-permute-start | bytes 393224
  343.5 19.8 %collective-permute-start.1 = (f32[16,2048]{1,0:T(8,128)S(1)}, f32[16,2048]{1,0:T(8,128)S(1)}, u32[]{:S(2)}, u32[]{:S(2)}) collective-permute-start(f32[16,2048]{1,0:T(8,128)S(1)} %fusion), channel_id=1, source_target_pairs={{0,2},{1,3},{2,4},{3,5},{4,6},{5,7},{6,8},{7,9},{8,10},{9,11},{10,... | collective-permute-start | bytes 393224
  344.8 22.9 %collective-permute-start.10 = (f32[16,2048]{1,0:T(8,128)S(1)}, f32[16,2048]{1,0:T(8,128)S(1)}, u32[]{:S(2)}, u32[]{:S(2)}) collective-permute-start(f32[16,2048]{1,0:T(8,128)S(1)} %fusion), channel_id=1, source_target_pairs={{0,11},{1,12},{2,13},{3,14},{4,15},{5,16},{6,17},{7,18},{8,19},{9,... | collective-permute-start | bytes 393224
  350.6 23.3 %collective-permute-start.11 = (f32[16,2048]{1,0:T(8,128)S(1)}, f32[16,2048]{1,0:T(8,128)S(1)}, u32[]{:S(2)}, u32[]{:S(2)}) collective-permute-start(f32[16,2048]{1,0:T(8,128)S(1)} %fusion), channel_id=1, source_target_pairs={{0,12},{1,13},{2,14},{3,15},{4,16},{5,17},{6,18},{7,19},{8,20},{9,... | collective-permute-start | bytes 393224
  354.6 20.6 %collective-permute-start.12 = (f32[16,2048]{1,0:T(8,128)S(1)}, f32[16,2048]{1,0:T(8,128)S(1)}, u32[]{:S(2)}, u32[]{:S(2)}) collective-permute-start(f32[16,2048]{1,0:T(8,128)S(1)} %fusion), channel_id=1, source_target_pairs={{0,13},{1,14},{2,15},{3,16},{4,17},{5,18},{6,19},{7,20},{8,21},{9,... | collective-permute-start | bytes 393224
  361.7 38.7 %copy-start.1 = (f32[16,2048]{1,0:T(8,128)}, f32[16,2048]{1,0:T(8,128)S(1)}, u32[]{:S(2)}) copy-start(f32[16,2048]{1,0:T(8,128)S(1)} %collective-permute-done) | copy-start | bytes 393220
  361.7 16.5 %collective-permute-start.13 = (f32[16,2048]{1,0:T(8,128)S(1)}, f32[16,2048]{1,0:T(8,128)S(1)}, u32[]{:S(2)}, u32[]{:S(2)}) collective-permute-start(f32[16,2048]{1,0:T(8,128)S(1)} %fusion), channel_id=1, source_target_pairs={{0,14},{1,15},{2,16},{3,17},{4,18},{5,19},{6,20},{7,21},{8,22},{9,... | collective-permute-start | bytes 393224
  363.3 38.9 %copy-start.2 = (f32[16,2048]{1,0:T(8,128)}, f32[16,2048]{1,0:T(8,128)S(1)}, u32[]{:S(2)}) copy-start(f32[16,2048]{1,0:T(8,128)S(1)} %collective-permute-done.1) | copy-start | bytes 393220
  363.3 19.4 %collective-permute-start.14 = (f32[16,2048]{1,0:T(8,128)S(1)}, f32[16,2048]{1,0:T(8,128)S(1)}, u32[]{:S(2)}, u32[]{:S(2)}) collective-permute-start(f32[16,2048]{1,0:T(8,128)S(1)} %fusion), channel_id=1, source_target_pairs={{0,15},{1,16},{2,17},{3,18},{4,19},{5,20},{6,21},{7,22},{8,23},{9,... | collective-permute-start | bytes 393224
  367.7 34.6 %copy-start.3 = (f32[16,2048]{1,0:T(8,128)}, f32[16,2048]{1,0:T(8,128)S(1)}, u32[]{:S(2)}) copy-start(f32[16,2048]{1,0:T(8,128)S(1)} %collective-permute-done.10) | copy-start | bytes 393220
  367.7 23.5 %collective-permute-start.2 = (f32[16,2048]{1,0:T(8,128)S(1)}, f32[16,2048]{1,0:T(8,128)S(1)}, u32[]{:S(2)}, u32[]{:S(2)}) collective-permute-start(f32[16,2048]{1,0:T(8,128)S(1)} %fusion), channel_id=1, source_target_pairs={{0,3},{1,4},{2,5},{3,6},{4,7},{5,8},{6,9},{7,10},{8,11},{9,12},{10... | collective-permute-start | bytes 393224
  373.8 28.4 %copy-start.4 = (f32[16,2048]{1,0:T(8,128)}, f32[16,2048]{1,0:T(8,128)S(1)}, u32[]{:S(2)}) copy-start(f32[16,2048]{1,0:T(8,128)S(1)} %collective-permute-done.11) | copy-start | bytes 393220
  373.9 20.3 %collective-permute-start.3 = (f32[16,2048]{1,0:T(8,128)S(1)}, f32[16,2048]{1,0:T(8,128)S(1)}, u32[]{:S(2)}, u32[]{:S(2)}) collective-permute-start(f32[16,2048]{1,0:T(8,128)S(1)} %fusion), channel_id=1, source_target_pairs={{0,4},{1,5},{2,6},{3,7},{4,8},{5,9},{6,10},{7,11},{8,12},{9,13},{1... | collective-permute-start | bytes 393224
  375.2 27.1 %copy-start.5 = (f32[16,2048]{1,0:T(8,128)}, f32[16,2048]{1,0:T(8,128)S(1)}, u32[]{:S(2)}) copy-start(f32[16,2048]{1,0:T(8,128)S(1)} %collective-permute-done.12) | copy-start | bytes 393220
  375.2 25.1 %collective-permute-start.4 = (f32[16,2048]{1,0:T(8,128)S(1)}, f32[16,2048]{1,0:T(8,128)S(1)}, u32[]{:S(2)}, u32[]{:S(2)}) collective-permute-start(f32[16,2048]{1,0:T(8,128)S(1)} %fusion), channel_id=1, source_target_pairs={{0,5},{1,6},{2,7},{3,8},{4,9},{5,10},{6,11},{7,12},{8,13},{9,14},{... | collective-permute-start | bytes 393224
  378.2 24.1 %copy-start.6 = (f32[16,2048]{1,0:T(8,128)}, f32[16,2048]{1,0:T(8,128)S(1)}, u32[]{:S(2)}) copy-start(f32[16,2048]{1,0:T(8,128)S(1)} %collective-permute-done.13) | copy-start | bytes 393220
  378.2 25.4 %collective-permute-start.5 = (f32[16,2048]{1,0:T(8,128)S(1)}, f32[16,2048]{1,0:T(8,128)}, u32[]{:S(2)}, u32[]{:S(2)}) collective-permute-start(f32[16,2048]{1,0:T(8,128)S(1)} %fusion), channel_id=1, source_target_pairs={{0,6},{1,7},{2,8},{3,9},{4,10},{5,11},{6,12},{7,13},{8,14},{9,15},... | collective-permute-start | bytes 393224
  382.8 19.5 %copy-start.7 = (f32[16,2048]{1,0:T(8,128)}, f32[16,2048]{1,0:T(8,128)S(1)}, u32[]{:S(2)}) copy-start(f32[16,2048]{1,0:T(8,128)S(1)} %collective-permute-done.14) | copy-start | bytes 393220
  382.8 20.9 %collective-permute-start.6 = (f32[16,2048]{1,0:T(8,128)S(1)}, f32[16,2048]{1,0:T(8,128)}, u32[]{:S(2)}, u32[]{:S(2)}) collective-permute-start(f32[16,2048]{1,0:T(8,128)S(1)} %fusion), channel_id=1, source_target_pairs={{0,7},{1,8},{2,9},{3,10},{4,11},{5,12},{6,13},{7,14},{8,15},{9,16}... | collective-permute-start | bytes 393224
  391.1 11.1 %copy-start.8 = (f32[16,2048]{1,0:T(8,128)}, f32[16,2048]{1,0:T(8,128)S(1)}, u32[]{:S(2)}) copy-start(f32[16,2048]{1,0:T(8,128)S(1)} %collective-permute-done.2) | copy-start | bytes 393220
  391.1 12.5 %collective-permute-start.7 = (f32[16,2048]{1,0:T(8,128)S(1)}, f32[16,2048]{1,0:T(8,128)}, u32[]{:S(2)}, u32[]{:S(2)}) collective-permute-start(f32[16,2048]{1,0:T(8,128)S(1)} %fusion), channel_id=1, source_target_pairs={{0,8},{1,9},{2,10},{3,11},{4,12},{5,13},{6,14},{7,15},{8,16},{9,17... | collective-permute-start | bytes 393224
  394.1 8.2 copy-start.9
  394.1 12.0 %collective-permute-start.8 = (f32[16,2048]{1,0:T(8,128)S(1)}, f32[16,2048]{1,0:T(8,128)}, u32[]{:S(2)}, u32[]{:S(2)}) collective-permute-start(f32[16,2048]{1,0:T(8,128)S(1)} %fusion), channel_id=1, source_target_pairs={{0,9},{1,10},{2,11},{3,12},{4,13},{5,14},{6,15},{7,16},{8,17},{9,1... | collective-permute-start | bytes 393224
  400.3 2.0 copy-start.10
  400.3 12.8 %collective-permute-start.9 = (f32[16,2048]{1,0:T(8,128)S(1)}, f32[16,2048]{1,0:T(8,128)}, u32[]{:S(2)}, u32[]{:S(2)}) collective-permute-start(f32[16,2048]{1,0:T(8,128)S(1)} %fusion), channel_id=1, source_target_pairs={{0,10},{1,11},{2,12},{3,13},{4,14},{5,15},{6,16},{7,17},{8,18},{9,... | collective-permute-start | bytes 393224
  442.2 407.7 %all-reduce.7.cloned.1.call-start = ((), (), s32[]{:S(2)}) async-start(), calls=%async_computation.2 | async-start | bytes 786432 | tf_op jit(solution)/shard_map/psum | solution.py:53
Sparse Core Ops, SparseCore 0:
  122.8 49.5 all-reduce.4
  442.4 294.0 all-gather.2
  804.5 45.3 all-reduce.6
